TPU v7x, 256 devices: a whole 4x4x8 slice. The times are simulated.
256 devices in a mesh: seq: 16 (over x, y_lo, core), ch: 16 (over z, y_hi).
Axes of the slice: x: 4, y: 4 (y_hi: 2, y_lo: 2; y = y_hi * 2 + y_lo), z: 8, core: 2. Of those that a mesh axis runs over, the one named last changes fastest.
Arguments:
- grad_out: bfloat16 [2048, 8192], P('seq', 'ch'), may hold values from -6 to 6
- out_weight: bfloat16 [8192, 8192], P('ch'), may hold values from -0.0625 to 0.0625
- query_gate: bfloat16 [2048, 8192], P('seq', 'ch'), may hold values from -6 to 6
- key_branch: bfloat16 [2048, 8192], P('seq', 'ch'), may hold values from -6 to 6
- value_branch: bfloat16 [2048, 8192], P('seq', 'ch'), may hold values from -6 to 6
- filter_taps: bfloat16 [2048, 8192], P('seq', 'ch'), may hold values from -4 to 4
Outputs:
- key_grad: bfloat16 [2048, 8192], P('seq', 'ch')
- value_grad: bfloat16 [2048, 8192], P('seq', 'ch')
- filter_grad: float32 [2048, 8192], P('seq', 'ch')
All inputs are finite; a program needn't handle non-finite values.
Results may differ from a plain program's by a relative error of at most 0.017.
Values may be sent and summed in bfloat16 or wider, within the bound.
A program may use at most 192 MiB of HBM per device.

v0:
```python
import math
import jax
import jax.numpy as jnp
from jax import lax
from jax.sharding import PartitionSpec as P


def build_tables(seg_len):
    twice_length = 2 * seg_len
    freq_index = jnp.arange(twice_length, dtype=jnp.int32)
    row_index = jnp.arange(seg_len, dtype=jnp.int32)
    angle_unit = 2.0 * math.pi / twice_length
    fwd_phase = (freq_index[:, None] * row_index[None, :] % twice_length).astype(
        jnp.float32
    ) * angle_unit
    back_phase = (freq_index[None, :] * (seg_len - row_index[:, None]) % twice_length).astype(
        jnp.float32
    ) * angle_unit
    window_pos = (freq_index + seg_len) % twice_length
    window_phase = (freq_index[None, :] * window_pos[:, None] % twice_length).astype(
        jnp.float32
    ) * angle_unit
    parity = jnp.where(freq_index % 2 == 0, 1.0, -1.0).astype(jnp.float32)[:, None]
    return (
        jnp.cos(fwd_phase).astype(jnp.bfloat16),
        jnp.sin(fwd_phase).astype(jnp.bfloat16),
        jnp.cos(back_phase).astype(jnp.bfloat16),
        jnp.sin(back_phase).astype(jnp.bfloat16),
        jnp.cos(window_phase).astype(jnp.bfloat16),
        jnp.sin(window_phase).astype(jnp.bfloat16),
        parity,
    )


def spectra(block_list, cosine_forward, sine_forward):
    cosine_piece = jnp.einsum(
        "qk,rkb->rqb", cosine_forward, block_list, preferred_element_type=jnp.float32
    )
    sine_piece = jnp.einsum(
        "qk,rkb->rqb", sine_forward, block_list, preferred_element_type=jnp.float32
    )
    return (cosine_piece, sine_piece)


def shards(grad_out, out_weight, query_gate, key_branch, value_branch, filter_taps):
    seg_len = query_gate.shape[0]
    channels = query_gate.shape[1]
    twice_length = 2 * seg_len
    segments = lax.axis_size("seq")
    my_index = lax.axis_index("seq")
    factor = 1.0 / math.sqrt(seg_len * segments)
    grad_mix = lax.dot_general(
        lax.all_gather(grad_out, "ch", axis=1, tiled=True),
        out_weight,
        (((1,), (1,)), ((), ())),
        preferred_element_type=jnp.float32,
    )
    gated_grad = (grad_mix * query_gate.astype(jnp.float32)).astype(jnp.bfloat16)
    conv_input = (key_branch.astype(jnp.float32) * value_branch.astype(jnp.float32)).astype(
        jnp.bfloat16
    )
    tables = build_tables(seg_len)
    (
        cosine_forward,
        sine_forward,
        cosine_backward,
        sine_backward,
        cosine_window,
        sine_window,
        parity,
    ) = tables
    all_taps = lax.all_gather(filter_taps, "seq", axis=0, tiled=True)
    tap_cos, tap_sin = spectra(
        all_taps.reshape(segments, seg_len, channels), cosine_forward, sine_forward
    )
    kern_cos = jnp.concatenate([jnp.zeros_like(tap_cos[:1]), tap_cos[:-1]], 0) + parity * tap_cos
    kern_sin = jnp.concatenate([jnp.zeros_like(tap_sin[:1]), tap_sin[:-1]], 0) + parity * tap_sin
    own_cos, own_sin = spectra(conv_input[None], cosine_forward, sine_forward)
    own_cos = own_cos[0]
    own_sin = own_sin[0]
    zero_spec = jnp.zeros((twice_length, channels), jnp.float32)
    initial = (zero_spec, zero_spec, jnp.zeros(((segments + 1) * seg_len, channels), jnp.float32))
    piece_data = lax.all_gather(gated_grad, "seq", axis=0, tiled=True)
    block_count = piece_data.shape[0] // seg_len
    seg_ids = jnp.arange(block_count, dtype=jnp.int32)
    block_list = piece_data.reshape(block_count, seg_len, channels)
    grad_cos, grad_sin = spectra(block_list, cosine_forward, sine_forward)
    lag_steps = seg_ids - my_index
    inside = seg_ids < segments
    live_mask = ((lag_steps >= 0) & inside).astype(jnp.float32)[:, None, None]
    lag_clip = jnp.clip(lag_steps, 0, segments - 1)
    lag_kcos = jnp.take(kern_cos, lag_clip, axis=0)
    lag_ksin = jnp.take(kern_sin, lag_clip, axis=0)
    running_real = jnp.sum(live_mask * (grad_cos * lag_kcos + grad_sin * lag_ksin), axis=0)
    running_imaginary = jnp.sum(live_mask * (grad_sin * lag_kcos - grad_cos * lag_ksin), axis=0)
    product_real = (own_cos * grad_cos + own_sin * grad_sin).astype(jnp.bfloat16)
    product_imaginary = (own_sin * grad_cos - own_cos * grad_sin).astype(jnp.bfloat16)
    windows = jnp.einsum(
        "an,hny->hay", cosine_window, product_real, preferred_element_type=jnp.float32
    ) - jnp.einsum(
        "an,hny->hay", sine_window, product_imaginary, preferred_element_type=jnp.float32
    )
    windows = windows * (live_mask / twice_length)

    def place(item_index, buffer):
        offset = lag_clip[item_index] * seg_len
        current = lax.dynamic_slice_in_dim(buffer, offset, twice_length, 0)
        return lax.dynamic_update_slice_in_dim(buffer, current + windows[item_index], offset, 0)

    buffer = lax.fori_loop(0, block_list.shape[0], place, initial[2])
    convolution_gradient = (
        jnp.dot(
            cosine_backward, running_real.astype(jnp.bfloat16), preferred_element_type=jnp.float32
        )
        - jnp.dot(
            sine_backward,
            running_imaginary.astype(jnp.bfloat16),
            preferred_element_type=jnp.float32,
        )
    ) / twice_length
    own_rows = lax.psum_scatter(
        buffer[seg_len:].astype(jnp.bfloat16), "seq", scatter_dimension=0, tiled=True
    ).astype(jnp.float32)
    filter_grad = own_rows * factor
    key_grad = (convolution_gradient * value_branch.astype(jnp.float32)).astype(jnp.bfloat16)
    value_grad = (convolution_gradient * key_branch.astype(jnp.float32)).astype(jnp.bfloat16)
    return (key_grad, value_grad, filter_grad)


def solution(mesh):
    return jax.shard_map(
        shards,
        mesh=mesh,
        in_specs=(
            P("seq", "ch"),
            P("ch", None),
            P("seq", "ch"),
            P("seq", "ch"),
            P("seq", "ch"),
            P("seq", "ch"),
        ),
        out_specs=(P("seq", "ch"), P("seq", "ch"), P("seq", "ch")),
        check_vma=False,
    )
```

profile of v0, /device:TPU:32, one launch (start us, length us, event | category | flops | bytes accessed | tf_op | source)
XLA Modules:
  0.0 391.5 jit_solution(9335437715561925159)
XLA Ops:
  8.7 88.9 %all-gather.4.cloned.1.call-done = bf16[128,8192]{1,0:T(8,128)(2,1)} async-done(((bf16[128,512]{1,0:T(8,128)(2,1)}), bf16[128,8192]{1,0:T(8,128)(2,1)}) %all-gather.4.cloned.1.call-update) | async-done | bytes 2097168 | tf_op jit(solution)/shard_map/all_gather | solution.py:53
  97.6 7.6 %fusion.22 = bf16[128,512]{1,0:T(8,128)(2,1)} fusion(bf16[128,8192]{1,0:T(8,128)(2,1)} %all-gather.4.cloned.1.call-done, bf16[512,8192]{1,0:T(8,128)(2,1)} %param.11, bf16[128,512]{1,0:T(8,128)(2,1)} %param.12), kind=kOutput, calls=%fused_computation.40 | convolution fusion | flops 1073938432 | bytes 10747904 | tf_op jit(solution)/shard_map/dot_general | solution.py:52
  106.8 25.7 %all-gather.8.cloned.1.call-done = bf16[2048,512]{1,0:T(8,128)(2,1)} async-done(((bf16[128,512]{1,0:T(8,128)(2,1)}), bf16[2048,512]{1,0:T(8,128)(2,1)}) %all-gather.8.cloned.1.call-update) | async-done | bytes 2097168 | tf_op jit(solution)/shard_map/all_gather | solution.py:72
  132.5 3.2 convolution_bitcast_fusion.1
  135.7 4.5 %slice.17 = f32[15,256,512]{2,1,0:T(8,128)} slice(f32[16,256,512]{2,1,0:T(8,128)S(1)} %convolution_bitcast_fusion.1), slice={[0:15], [0:256], [0:512]} | slice | bytes 15728640 | tf_op jit(solution)/shard_map/slice | solution.py:76
  142.0 3.2 copy-done.1
  145.2 4.6 %slice.18 = f32[15,256,512]{2,1,0:T(8,128)} slice(f32[16,256,512]{2,1,0:T(8,128)S(1)} %convolution_bitcast_fusion), slice={[0:15], [0:256], [0:512]} | slice | bytes 15728640 | tf_op jit(solution)/shard_map/slice | solution.py:77
  149.8 18.9 %multiply_add_fusion.1 = (f32[16,256,512]{2,1,0:T(8,128)}, f32[16,256,512]{2,1,0:T(8,128)}) fusion(f32[16,256,512]{2,1,0:T(8,128)} %copy-done, f32[15,256,512]{2,1,0:T(8,128)} %slice.17, f32[256]{0:T(256)S(1)} %compare_select_fusion.3, f32[16,256,512]{2,1,0:T(8,128)} %copy-done.1, f32[15,256,512]{2,1,0:T(8,128)} %slice.18), kind=kLoop, calls=%fused_computation.25 | loop fusion | flops 8388608 | bytes 49284096 | tf_op jit(solution)/shard_map/add | solution.py:76
  168.7 7.7 %gather_fusion = f32[16,256,512]{2,1,0:T(8,128)} fusion(f32[16,256,512]{2,1,0:T(8,128)} %get-tuple-element.108, s32[1024]{0:T(1024)S(1)} %pad_clamp_fusion), kind=kCustom, calls=%fused_computation.clone | custom fusion | bytes 16777280 | tf_op jit(solution)/shard_map/jit(_take)/gather | solution.py:92
  176.4 9.2 %copy.18 = f32[16,256,512]{1,2,0:T(8,128)} copy(f32[16,256,512]{2,1,0:T(8,128)} %gather_fusion) | data formatting | bytes 16777216 | tf_op jit(solution)/shard_map/jit(_take)/gather | solution.py:92
  185.7 7.7 %gather_fusion.1 = f32[16,256,512]{2,1,0:T(8,128)} fusion(f32[16,256,512]{2,1,0:T(8,128)} %get-tuple-element.109, s32[1024]{0:T(1024)S(1)} %pad_clamp_fusion), kind=kCustom, calls=%fused_computation.1.clone | custom fusion | bytes 16777280 | tf_op jit(solution)/shard_map/jit(_take)/gather | solution.py:93
  193.3 9.3 %copy.20 = f32[16,256,512]{1,2,0:T(8,128)} copy(f32[16,256,512]{2,1,0:T(8,128)} %gather_fusion.1) | data formatting | bytes 16777216 | tf_op jit(solution)/shard_map/jit(_take)/gather | solution.py:93
  202.6 3.5 fusion.57
  206.1 10.9 %fusion.6 = (bf16[256,512]{0,1:T(8,128)(2,1)S(1)}, bf16[256,512]{0,1:T(8,128)(2,1)S(1)}, f32[16,512,256]{2,1,0:T(8,128)}) fusion(f32[16,512,256]{2,1,0:T(8,128)S(1)} %fusion.57, f32[16,256,512]{1,2,0:T(8,128)} %copy.20, f32[16,256,512]{1,2,0:T(8,128)} %copy.18, f32[16]{0:T(128)S(1)} %get-tuple-element.114, pred[16]{0:T(512)(128)(4,1)S(1)} %get-tuple-element.113, ...), kind=kOutput, calls=%fused_computation.14 | convolution fusion | flops 562266112 | bytes 36175952 | tf_op jit(solution)/shard_map/qk,rkb->rqb/dot_general | solution.py:39
  217.0 9.5 %fusion.11 = f32[16,512,256]{2,1,0:T(8,128)} fusion(f32[16,512,256]{2,1,0:T(8,128)} %get-tuple-element.110, f32[16,512,256]{2,1,0:T(8,128)S(1)} %fusion.57, f32[256,512]{0,1:T(8,128)S(1)} %convolution_bitcast_fusion.2, f32[256,512]{0,1:T(8,128)S(1)} %convolution_bitcast_fusion.3, s32[256]{0:T(256)S(1)} %and_select_fusion), kind=kOutput, calls=%fused_computation.26 | convolution fusion | flops 1083113472 | bytes 26215424 | tf_op jit(solution)/shard_map/an,hny->hay/dot_general | solution.py:100
  226.4 11.8 %multiply_bitcast_fusion = f32[16,256,512]{1,2,0:T(8,128)} fusion(f32[16,512,256]{2,1,0:T(8,128)} %fusion.11, f32[16]{0:T(128)S(1)} %broadcast_select_fusion, f32[16,512,256]{2,1,0:T(8,128)} %get-tuple-element.110, f32[16,512,256]{2,1,0:T(8,128)S(1)} %fusion.57, f32[256,512]{0,1:T(8,128)S(1)} %convolution_bitcast_fusion.2, ...), kind=kOutput, calls=%fused_computation.23 | convolution fusion | flops 1087307776 | bytes 34604096 | tf_op jit(solution)/shard_map/an,hny->hay/dot_general | solution.py:98
  238.3 2.6 broadcast_in_dim.30
  240.9 71.4 %while.13 = (s32[]{:T(128)}, f32[2176,512]{1,0:T(8,128)}, s32[16]{0:T(128)S(1)}, f32[16,256,512]{1,2,0:T(8,128)}, s32[]{:T(128)}, /*index=5*/s32[1]{0:T(128)}, s32[]{:T(128)}, s32[]{:T(128)}) while((s32[]{:T(128)}, f32[2176,512]{1,0:T(8,128)}, s32[16]{0:T(128)S(1)}, f32[16,256,512]{1,2,0:T(8,128)}, s32[]{:T(128)}, /*index=5*/s32[1]{0:T(128)}, ...), condition=%wide.region_3.5_spmd, body=%wide.region_2.4_spmd.sunk | while | flops 131078 | bytes 3670167 | solution.py:110
  247.9 1.9 fusion.115
  252.3 1.9 fusion.115
  256.8 1.9 fusion.115
  261.2 2.0 fusion.115
  265.7 1.9 fusion.115
  270.2 1.9 fusion.115
  274.7 1.9 fusion.115
  279.1 1.9 fusion.115
  283.6 1.9 fusion.115
  288.1 1.9 fusion.115
  297.0 1.9 fusion.115
  301.4 1.9 fusion.115
  312.3 3.8 slice.21
  318.2 65.2 %reduce-scatter.2.cloned.1.call-done = bf16[128,512]{1,0:T(8,128)(2,1)} async-done(((bf16[2048,512]{1,0:T(8,128)(2,1)}), bf16[128,512]{1,0:T(8,128)(2,1)}) %reduce-scatter.2.cloned.1.call-update) | async-done | bytes 131088 | tf_op jit(solution)/shard_map/reduce_scatter | solution.py:121
  (85 shorter events, 45.9 us)
Async XLA Ops:
  7.2 98.2 %copy-start.4 = (bf16[128,512]{1,0:T(8,128)(2,1)S(1)}, bf16[128,512]{1,0:T(8,128)(2,1)}, u32[]{:S(2)}) copy-start(bf16[128,512]{1,0:T(8,128)(2,1)} %param.13) | copy-start | bytes 393220
  7.2 98.2 %copy-start.5 = (bf16[128,512]{1,0:T(8,128)(2,1)S(1)}, bf16[128,512]{1,0:T(8,128)(2,1)}, u32[]{:S(2)}) copy-start(bf16[128,512]{1,0:T(8,128)(2,1)} %param.14) | copy-start | bytes 393220
  7.2 90.4 %all-gather.4.cloned.1.call-start = ((), (), s32[]{:S(2)}) async-start(), calls=%async_computation.1 | async-start | bytes 2228224 | tf_op jit(solution)/shard_map/all_gather | solution.py:53
  7.9 124.6 %all-gather.8.cloned.1.call-start = ((), (), s32[]{:S(2)}) async-start(), calls=%async_computation.3 | async-start | bytes 2228224 | tf_op jit(solution)/shard_map/all_gather | solution.py:72
  8.7 193.9 %all-gather.6.cloned.1.call-start = ((), (), s32[]{:S(2)}) async-start(), calls=%async_computation.2 | async-start | bytes 2228224 | tf_op jit(solution)/shard_map/all_gather | solution.py:83
  105.2 278.1 %reduce-scatter.2.cloned.1.call-start = ((), (), s32[]{:S(2)}) async-start(), calls=%async_computation.4 | async-start | bytes 2228224 | tf_op jit(solution)/shard_map/reduce_scatter | solution.py:121
  135.7 6.2 %copy-start = (f32[16,256,512]{2,1,0:T(8,128)}, f32[16,256,512]{2,1,0:T(8,128)S(1)}, u32[]{:S(2)}) copy-start(f32[16,256,512]{2,1,0:T(8,128)S(1)} %convolution_bitcast_fusion.1) | copy-start | bytes 25165828
  135.7 4.6 %copy-start.2 = (bf16[2048,512]{1,0:T(8,128)(2,1)S(1)}, bf16[2048,512]{1,0:T(8,128)(2,1)}, u32[]{:S(2)}) copy-start(bf16[2048,512]{1,0:T(8,128)(2,1)} %all-gather.8.cloned.1.call-done) | copy-start | bytes 6291460
  141.9 3.2 copy-start.1
  202.6 3.5 copy-start.3
Sparse Core Ops, SparseCore 0:
  10.5 87.1 all-gather.3
  99.5 32.9 all-gather.7
  134.9 36.3 all-gather.5
  316.2 67.0 reduce-scatter.1
where the time goes:
time: 394 us; the launch traced here: 392 us
  waiting for transfers between devices  181 us (46%)
  local copies, waits for them, and re-layouts  82.5 us (21%)
  matrix products  51.6 us (13%)
  other arithmetic  51.5 us (13%)
  between operations  13.9 us (4%)
  loops' own time  10.7 us (3%)
    all_gather x1, waiting for transfers between devices, shards(): lax.all_gather(grad_out, 'ch', axis=1, tiled=True)  88.9 us
    reduce_scatter x1, waiting for transfers between devices, shards(): lax.psum_scatter(buffer[seg_len:].astype(jnp.bfloat16), 'seq', scatter_di...  65.2 us
    dynamic_update_slice x16, other arithmetic, place(): lax.dynamic_update_slice_in_dim(buffer, current + windows[item_index], of...  30.9 us
    all_gather x1, waiting for transfers between devices, shards(): all_taps = lax.all_gather(filter_taps, 'seq', axis=0, tiled=True)  25.7 us
    dynamic_slice x32, local copies, waits for them, and re-layouts, place(): windows[item_index]  20.5 us
    add x1, other arithmetic, shards(): jnp.concatenate([jnp.zeros_like(tap_cos[:1]), tap_cos[:-1]], 0)  18.9 us
    gather x2, local copies, waits for them, and re-layouts, shards(): lag_kcos = jnp.take(kern_cos, lag_clip, axis=0)  17 us
    gather x2, local copies, waits for them, and re-layouts, shards(): lag_ksin = jnp.take(kern_sin, lag_clip, axis=0)  16.9 us
  transfers between devices with their start and end apart: 4, of which 3 were waited for; matrix products, arithmetic and copies ran while one was open for 20% of the time, Pallas kernels for 0%

commit v1 on v0

--- a/solution.py
+++ b/solution.py
@@ -69,7 +69,9 @@
         sine_window,
         parity,
     ) = tables
-    all_taps = lax.all_gather(filter_taps, "seq", axis=0, tiled=True)
+    all_taps = jnp.concatenate(
+        lax.all_to_all(jnp.stack([filter_taps] * lax.axis_size("seq")), "seq", 0, 0), axis=0
+    )
     tap_cos, tap_sin = spectra(
         all_taps.reshape(segments, seg_len, channels), cosine_forward, sine_forward
     )

time: 394 us -> 378 us (0.959)
  waiting for transfers between devices: 181 us -> 158 us
  starting transfers between devices: 0.16 us -> 5.54 us
    all_gather x1 -> x0, waiting for transfers between devices: 25.7 us -> none  [shards(): all_taps = lax.all_gather(filter_taps, 'seq', axis=0, tiled=True)]
    all_gather x1, waiting for transfers between devices: 88.9 us -> 95.8 us  [shards(): lax.all_gather(grad_out, 'ch', axis=1, tiled=True)]
    all_to_all x0 -> x1, starting transfers between devices: none -> 5.42 us  [shards(): lax.all_to_all(jnp.stack([filter_taps] * lax.axis_size('seq')), 'seq', 0, 0)]
  transfers between devices with their start and end apart: 4 -> 4, of which waited for: 3 -> 2; matrix products, arithmetic and copies ran while one was open for 20% -> 21% of each run, Pallas kernels for 0% -> 0%
where the time goes in v1:
time: 378 us; the launch traced here: 375 us
  waiting for transfers between devices  158 us (42%)
  local copies, waits for them, and re-layouts  85.3 us (23%)
  other arithmetic  51.6 us (14%)
  matrix products  50 us (13%)
  between operations  13.9 us (4%)
  loops' own time  10.7 us (3%)
  starting transfers between devices  5.54 us (1%)
    all_gather x1, waiting for transfers between devices, shards(): lax.all_gather(grad_out, 'ch', axis=1, tiled=True)  95.8 us
    reduce_scatter x1, waiting for transfers between devices, shards(): lax.psum_scatter(buffer[seg_len:].astype(jnp.bfloat16), 'seq', scatter_di...  61.7 us
    dynamic_update_slice x16, other arithmetic, place(): lax.dynamic_update_slice_in_dim(buffer, current + windows[item_index], of...  30.9 us
    dynamic_slice x32, local copies, waits for them, and re-layouts, place(): windows[item_index]  20.5 us
    add x1, other arithmetic, shards(): jnp.concatenate([jnp.zeros_like(tap_cos[:1]), tap_cos[:-1]], 0)  19 us
    gather x2, local copies, waits for them, and re-layouts, shards(): lag_ksin = jnp.take(kern_sin, lag_clip, axis=0)  16.9 us
    gather x2, local copies, waits for them, and re-layouts, shards(): lag_kcos = jnp.take(kern_cos, lag_clip, axis=0)  16.9 us
    dot_general x3, matrix products, spectra(): jnp.einsum('qk,rkb->rqb', sine_forward, block_list, preferred_element_typ...  13.3 us
  transfers between devices with their start and end apart: 4, of which 2 were waited for; matrix products, arithmetic and copies ran while one was open for 21% of the time, Pallas kernels for 0%

profile of v1, /device:TPU:32, one launch (start us, length us, event | category | flops | bytes accessed | tf_op | source)
XLA Modules:
  0.0 375.3 jit_solution(4942925238591469975)
XLA Ops:
  7.9 2.5 stack.2
  10.4 5.4 %all-to-all-start = ((bf16[16,128,512]{2,1,0:T(8,128)(2,1)}), bf16[16,128,512]{2,1,0:T(8,128)(2,1)S(1)}, u32[]{:S(2)}, u32[]{:S(2)}) async-start(bf16[16,128,512]{2,1,0:T(8,128)(2,1)} %stack.2), calls=%async_computation | async-start | bytes 4194304 | tf_op jit(solution)/shard_map/all_to_all | solution.py:73
  15.9 95.8 %all-gather.3.cloned.1.call-done = bf16[128,8192]{1,0:T(8,128)(2,1)} async-done(((bf16[128,512]{1,0:T(8,128)(2,1)}), bf16[128,8192]{1,0:T(8,128)(2,1)}) %all-gather.3.cloned.1.call-update) | async-done | bytes 2097168 | tf_op jit(solution)/shard_map/all_gather | solution.py:53
  111.7 7.6 %fusion.22 = bf16[128,512]{1,0:T(8,128)(2,1)} fusion(bf16[128,8192]{1,0:T(8,128)(2,1)} %all-gather.3.cloned.1.call-done, bf16[512,8192]{1,0:T(8,128)(2,1)} %param.11, bf16[128,512]{1,0:T(8,128)(2,1)} %param.12), kind=kOutput, calls=%fused_computation.40 | convolution fusion | flops 1073938432 | bytes 10747904 | tf_op jit(solution)/shard_map/dot_general | solution.py:52
  122.6 5.0 %slice.17 = f32[15,256,512]{2,1,0:T(8,128)} slice(f32[16,256,512]{2,1,0:T(8,128)S(1)} %convolution_bitcast_fusion.1), slice={[0:15], [0:256], [0:512]} | slice | bytes 15728640 | tf_op jit(solution)/shard_map/slice | solution.py:78
  129.3 3.2 copy-done.1
  132.5 4.6 %slice.18 = f32[15,256,512]{2,1,0:T(8,128)} slice(f32[16,256,512]{2,1,0:T(8,128)S(1)} %convolution_bitcast_fusion), slice={[0:15], [0:256], [0:512]} | slice | bytes 15728640 | tf_op jit(solution)/shard_map/slice | solution.py:79
  137.1 19.0 %multiply_add_fusion.1 = (f32[16,256,512]{2,1,0:T(8,128)}, f32[16,256,512]{2,1,0:T(8,128)}) fusion(f32[16,256,512]{2,1,0:T(8,128)} %copy-done, f32[15,256,512]{2,1,0:T(8,128)} %slice.17, f32[256]{0:T(256)S(1)} %compare_select_fusion.3, f32[16,256,512]{2,1,0:T(8,128)} %copy-done.1, f32[15,256,512]{2,1,0:T(8,128)} %slice.18), kind=kLoop, calls=%fused_computation.25 | loop fusion | flops 8388608 | bytes 49284096 | tf_op jit(solution)/shard_map/add | solution.py:78
  156.1 7.7 %gather_fusion = f32[16,256,512]{2,1,0:T(8,128)} fusion(f32[16,256,512]{2,1,0:T(8,128)} %get-tuple-element.108, s32[1024]{0:T(1024)S(1)} %pad_clamp_fusion), kind=kCustom, calls=%fused_computation.clone | custom fusion | bytes 16777280 | tf_op jit(solution)/shard_map/jit(_take)/gather | solution.py:94
  163.7 9.2 %copy.18 = f32[16,256,512]{1,2,0:T(8,128)} copy(f32[16,256,512]{2,1,0:T(8,128)} %gather_fusion) | data formatting | bytes 16777216 | tf_op jit(solution)/shard_map/jit(_take)/gather | solution.py:94
  173.0 7.7 %gather_fusion.1 = f32[16,256,512]{2,1,0:T(8,128)} fusion(f32[16,256,512]{2,1,0:T(8,128)} %get-tuple-element.109, s32[1024]{0:T(1024)S(1)} %pad_clamp_fusion), kind=kCustom, calls=%fused_computation.1.clone | custom fusion | bytes 16777280 | tf_op jit(solution)/shard_map/jit(_take)/gather | solution.py:95
  180.6 9.3 %copy.20 = f32[16,256,512]{1,2,0:T(8,128)} copy(f32[16,256,512]{2,1,0:T(8,128)} %gather_fusion.1) | data formatting | bytes 16777216 | tf_op jit(solution)/shard_map/jit(_take)/gather | solution.py:95
  189.9 3.5 fusion.57
  193.4 10.9 %fusion.6 = (bf16[256,512]{0,1:T(8,128)(2,1)S(1)}, bf16[256,512]{0,1:T(8,128)(2,1)S(1)}, f32[16,512,256]{2,1,0:T(8,128)}) fusion(f32[16,512,256]{2,1,0:T(8,128)S(1)} %fusion.57, f32[16,256,512]{1,2,0:T(8,128)} %copy.20, f32[16,256,512]{1,2,0:T(8,128)} %copy.18, f32[16]{0:T(128)S(1)} %get-tuple-element.112, pred[16]{0:T(512)(128)(4,1)S(1)} %get-tuple-element.111, ...), kind=kOutput, calls=%fused_computation.14 | convolution fusion | flops 562266112 | bytes 36175952 | tf_op jit(solution)/shard_map/qk,rkb->rqb/dot_general | solution.py:39
  204.3 9.5 %fusion.11 = f32[16,512,256]{2,1,0:T(8,128)} fusion(f32[16,512,256]{2,1,0:T(8,128)} %get-tuple-element.110, f32[16,512,256]{2,1,0:T(8,128)S(1)} %fusion.57, f32[256,512]{0,1:T(8,128)S(1)} %convolution_bitcast_fusion.2, f32[256,512]{0,1:T(8,128)S(1)} %convolution_bitcast_fusion.3, s32[256]{0:T(256)S(1)} %and_select_fusion), kind=kOutput, calls=%fused_computation.26 | convolution fusion | flops 1083113472 | bytes 26215424 | tf_op jit(solution)/shard_map/an,hny->hay/dot_general | solution.py:102
  213.7 11.8 %multiply_bitcast_fusion = f32[16,256,512]{1,2,0:T(8,128)} fusion(f32[16,512,256]{2,1,0:T(8,128)} %fusion.11, f32[16]{0:T(128)S(1)} %broadcast_select_fusion, f32[16,512,256]{2,1,0:T(8,128)} %get-tuple-element.110, f32[16,512,256]{2,1,0:T(8,128)S(1)} %fusion.57, f32[256,512]{0,1:T(8,128)S(1)} %convolution_bitcast_fusion.2, ...), kind=kOutput, calls=%fused_computation.23 | convolution fusion | flops 1087307776 | bytes 34604096 | tf_op jit(solution)/shard_map/an,hny->hay/dot_general | solution.py:100
  225.5 2.6 broadcast_in_dim.30
  228.1 71.4 %while.13 = (s32[]{:T(128)}, f32[2176,512]{1,0:T(8,128)}, s32[16]{0:T(128)S(1)}, f32[16,256,512]{1,2,0:T(8,128)}, s32[]{:T(128)}, /*index=5*/s32[1]{0:T(128)}, s32[]{:T(128)}, s32[]{:T(128)}) while((s32[]{:T(128)}, f32[2176,512]{1,0:T(8,128)}, s32[16]{0:T(128)S(1)}, f32[16,256,512]{1,2,0:T(8,128)}, s32[]{:T(128)}, /*index=5*/s32[1]{0:T(128)}, ...), condition=%wide.region_3.5_spmd, body=%wide.region_2.4_spmd.sunk | while | flops 131078 | bytes 3670167 | solution.py:112
  230.7 1.9 fusion.115
  235.1 1.9 fusion.115
  239.6 1.9 fusion.115
  244.1 1.9 fusion.115
  248.5 1.9 fusion.115
  257.4 1.9 fusion.115
  266.3 1.9 fusion.115
  270.8 1.9 fusion.115
  275.3 1.9 fusion.115
  279.7 1.9 fusion.115
  284.2 1.9 fusion.115
  288.7 1.9 fusion.115
  299.5 3.8 %slice.21 = bf16[2048,512]{1,0:T(8,128)(2,1)} slice(f32[2176,512]{1,0:T(8,128)} %get-tuple-element.83), slice={[128:2176], [0:512]} | slice | bytes 4194304 | tf_op jit(solution)/shard_map/slice | solution.py:124
  305.4 61.7 %reduce-scatter.2.cloned.1.call-done = bf16[128,512]{1,0:T(8,128)(2,1)} async-done(((bf16[2048,512]{1,0:T(8,128)(2,1)}), bf16[128,512]{1,0:T(8,128)(2,1)}) %reduce-scatter.2.cloned.1.call-update) | async-done | bytes 131088 | tf_op jit(solution)/shard_map/reduce_scatter | solution.py:123
  (84 shorter events, 46.8 us)
Async XLA Ops:
  7.2 104.5 %all-gather.3.cloned.1.call-start = ((), (), s32[]{:S(2)}) async-start(), calls=%async_computation.2 | async-start | bytes 2228224 | tf_op jit(solution)/shard_map/all_gather | solution.py:53
  7.9 111.5 %copy-start.3 = (bf16[128,512]{1,0:T(8,128)(2,1)S(1)}, bf16[128,512]{1,0:T(8,128)(2,1)}, u32[]{:S(2)}) copy-start(bf16[128,512]{1,0:T(8,128)(2,1)} %param.13) | copy-start | bytes 393220
  7.9 111.5 %copy-start.4 = (bf16[128,512]{1,0:T(8,128)(2,1)S(1)}, bf16[128,512]{1,0:T(8,128)(2,1)}, u32[]{:S(2)}) copy-start(bf16[128,512]{1,0:T(8,128)(2,1)} %param.14) | copy-start | bytes 393220
  10.4 110.5 %all-to-all-start = ((bf16[16,128,512]{2,1,0:T(8,128)(2,1)}), bf16[16,128,512]{2,1,0:T(8,128)(2,1)S(1)}, u32[]{:S(2)}, u32[]{:S(2)}) async-start(bf16[16,128,512]{2,1,0:T(8,128)(2,1)} %stack.2), calls=%async_computation | async-start | bytes 4194304 | tf_op jit(solution)/shard_map/all_to_all | solution.py:73
  15.8 174.1 %all-gather.5.cloned.1.call-start = ((), (), s32[]{:S(2)}) async-start(), calls=%async_computation.3 | async-start | bytes 2228224 | tf_op jit(solution)/shard_map/all_gather | solution.py:85
  119.3 247.9 %reduce-scatter.2.cloned.1.call-start = ((), (), s32[]{:S(2)}) async-start(), calls=%async_computation.4 | async-start | bytes 2228224 | tf_op jit(solution)/shard_map/reduce_scatter | solution.py:123
  122.6 6.6 %copy-start = (f32[16,256,512]{2,1,0:T(8,128)}, f32[16,256,512]{2,1,0:T(8,128)S(1)}, u32[]{:S(2)}) copy-start(f32[16,256,512]{2,1,0:T(8,128)S(1)} %convolution_bitcast_fusion.1) | copy-start | bytes 25165828
  129.3 3.2 copy-start.1
  189.9 3.5 copy-start.2
Sparse Core Ops, SparseCore 0:
  10.4 101.2 all-gather.2
  119.4 32.9 all-gather.4
  303.5 63.6 reduce-scatter.1
